TPU v7x, 512 devices: a whole 4x4x16 slice. The times are simulated.
512 devices in a mesh: energy: 32 (over z, core), slab: 16 (over y, x).
Axes of the slice: x: 4, y: 4, z: 16, core: 2. Of those that a mesh axis runs over, the one named last changes fastest.
Arguments:
- retarded: bfloat16 [16, 768, 2, 128, 128], P('slab', 'energy'), may hold values from -0.5 to 0.5
- self_lesser: bfloat16 [16, 768, 2, 128, 128], P('slab', 'energy'), may hold values from -6 to 6
- coupling: bfloat16 [4, 2, 128, 128], replicated, may hold values from -0.1875 to 0.1875
- occupancy: float32 [4], replicated, may hold values from 0.2 to 4
- adaptive_owner: int32 [384], replicated, may hold values from 0 to 31, as said below
- phonon_offsets: int32 [4], replicated, may hold values from 1 to 12, as said below
Outputs:
- phonon_lesser: float32 [16, 384, 2, 128, 128], P('slab', 'energy')
Inputs may be any that keep to these rules, and one draw needn't show every extreme that they name: `adaptive_owner`: each energy device holds at least one and at most 24 energies, and one or more hold exactly 24. Of the 12 energies e that share e // 12, no device holds more than 1, and some device holds exactly 1 of some such block. `phonon_offsets`: one of the offsets equals 12 and another one equals 1.
All inputs are finite; a program needn't handle non-finite values.
Results may differ from a plain program's by a relative error of at most 0.0064.
Values may be sent and summed in bfloat16 or wider, within the bound.
A program may use at most 64 MiB of HBM per device.

v0:
```python
import jax
import jax.numpy as jnp
from jax import lax
from jax.sharding import PartitionSpec as P


def with_halo(array, sides, width, wrap):
    for axis, dim in sides:
        peers, length = (lax.axis_size(axis), array.shape[dim])
        up = [(i, (i + 1) % peers) for i in range(peers if wrap else peers - 1)]
        down = [(j, i) for i, j in up]
        last = lax.slice_in_dim(array, length - width, length, axis=dim)
        initial = lax.slice_in_dim(array, 0, width, axis=dim)
        before = lax.ppermute(last, axis, up)
        after = lax.ppermute(initial, axis, down)
        array = jnp.concatenate([before, array, after], axis=dim)
    return array


def batched(left_block, right_block):
    return jnp.einsum("jab,jbc->jac", left_block, right_block, preferred_element_type=jnp.float32)


def batched_transposed(left_block, right_block):
    return jnp.einsum("jab,jcb->jac", left_block, right_block, preferred_element_type=jnp.float32)


def lesser_blocks(green_ret, sigma_total):
    ret_real, ret_imag = (green_ret[:, 0], green_ret[:, 1])
    sig_real, sig_imag = (sigma_total[:, 0], sigma_total[:, 1])
    half_real = batched(ret_real, sig_real) - batched(ret_imag, sig_imag)
    half_imag = batched(ret_real, sig_imag) + batched(ret_imag, sig_real)
    half_product = jnp.stack([half_real, half_imag], 1).astype(jnp.bfloat16)
    hp_real, hp_imag = (half_product[:, 0], half_product[:, 1])
    out_real = batched_transposed(hp_real, ret_real) + batched_transposed(hp_imag, ret_imag)
    out_imag = batched_transposed(hp_imag, ret_real) - batched_transposed(hp_real, ret_imag)
    return jnp.stack([out_real, out_imag], 1).astype(jnp.bfloat16)


def combined(stacked_rims):
    own_sigma = stacked_rims[1].astype(jnp.float32)
    beside = stacked_rims[0].astype(jnp.float32) + stacked_rims[2].astype(jnp.float32)
    return (own_sigma + 0.5 * beside).astype(jnp.bfloat16)


def sandwich(coupling_mode, weighted):
    m_real, m_imag = (coupling_mode[0], coupling_mode[1])
    w_real, w_imag = (weighted[:, 0], weighted[:, 1])
    left_real = jnp.einsum(
        "ab,jbc->jac", m_real, w_real, preferred_element_type=jnp.float32
    ) - jnp.einsum("ab,jbc->jac", m_imag, w_imag, preferred_element_type=jnp.float32)
    left_imag = jnp.einsum(
        "ab,jbc->jac", m_real, w_imag, preferred_element_type=jnp.float32
    ) + jnp.einsum("ab,jbc->jac", m_imag, w_real, preferred_element_type=jnp.float32)
    coupled = jnp.stack([left_real, left_imag], 1).astype(jnp.bfloat16)
    c_real, c_imag = (coupled[:, 0], coupled[:, 1])
    out_real = jnp.einsum(
        "jab,cb->jac", c_real, m_real, preferred_element_type=jnp.float32
    ) + jnp.einsum("jab,cb->jac", c_imag, m_imag, preferred_element_type=jnp.float32)
    out_imag = jnp.einsum(
        "jab,cb->jac", c_imag, m_real, preferred_element_type=jnp.float32
    ) - jnp.einsum("jab,cb->jac", c_real, m_imag, preferred_element_type=jnp.float32)
    return jnp.stack([out_real, out_imag], 1)


def body(retarded, self_lesser, coupling, occupancy, adaptive_owner, phonon_offsets):
    n_energy = lax.axis_size("energy")
    my_index = lax.axis_index("energy")
    energies = adaptive_owner.shape[0]
    per_device = energies // n_energy
    capacity = retarded.shape[1]
    slot_count = -(-capacity // n_energy)
    positions = jnp.arange(energies, dtype=jnp.int32)
    block_of = positions // per_device
    same_owner = adaptive_owner[:, None] == adaptive_owner[None, :]
    earlier = same_owner & (positions[None, :] < positions[:, None])
    slot_rank = jnp.sum(earlier.astype(jnp.int32), axis=1)
    same_block = block_of[None, :] == block_of[:, None]
    group_rank = jnp.sum((earlier & same_block).astype(jnp.int32), axis=1)
    target = block_of * slot_count + group_rank
    targets = jnp.arange(n_energy * slot_count, dtype=jnp.int32)
    matches = (adaptive_owner == my_index)[None, :] & (target[None, :] == targets[:, None])
    send_slot = jnp.sum(jnp.where(matches, slot_rank[None, :], 0), axis=1)
    first_energy = my_index * per_device
    own_owner = lax.dynamic_slice_in_dim(adaptive_owner, first_energy, per_device)
    own_rank = lax.dynamic_slice_in_dim(group_rank, first_energy, per_device)
    receive_slot = own_owner * slot_count + own_rank
    stacked_rims = with_halo(self_lesser, (("slab", 0),), 1, False)
    formed = lesser_blocks(retarded[0], combined(stacked_rims))
    outgoing = jnp.take(formed, send_slot, axis=0)
    arrived = lax.all_to_all(outgoing, "energy", split_axis=0, concat_axis=0, tiled=True)
    lesser = jnp.take(arrived, receive_slot, axis=0)
    widened = with_halo(lesser, (("energy", 0),), per_device, True)
    accumulated = jnp.zeros((per_device, 2, lesser.shape[2], lesser.shape[3]), jnp.float32)
    for phonon_mode in range(coupling.shape[0]):
        offset = phonon_offsets[phonon_mode]
        shifted_up = lax.dynamic_slice_in_dim(widened, per_device + offset, per_device, 0).astype(
            jnp.float32
        )
        shifted_down = lax.dynamic_slice_in_dim(widened, per_device - offset, per_device, 0).astype(
            jnp.float32
        )
        weight_one = occupancy[phonon_mode]
        weighted = ((weight_one + 1.0) * shifted_up + weight_one * shifted_down).astype(
            jnp.bfloat16
        )
        accumulated = accumulated + sandwich(coupling[phonon_mode], weighted)
    return accumulated[None]


def solution(mesh):
    placed = (
        P("slab", "energy", None, None, None),
        P("slab", "energy", None, None, None),
        P(),
        P(),
        P(),
        P(),
    )
    return jax.shard_map(
        body,
        mesh=mesh,
        in_specs=placed,
        out_specs=P("slab", "energy", None, None, None),
        check_vma=False,
    )
```

profile of v0, /device:TPU:1, one launch (start us, length us, event | category | flops | bytes accessed | tf_op | source)
XLA Modules:
  0.0 208.1 jit_solution(3930400108057080456)
XLA Ops:
  0.0 1.9 copy.48
  1.9 5.1 %collective-permute-start = (bf16[1,24,2,128,128]{3,4,1,2,0:T(8,128)(2,1)S(1)}, bf16[1,24,2,128,128]{3,4,1,2,0:T(8,128)(2,1)}, u32[]{:S(2)}, u32[]{:S(2)}) collective-permute-start(bf16[1,24,2,128,128]{3,4,1,2,0:T(8,128)(2,1)S(1)} %copy.48), channel_id=1, source_target_pairs={{0,1},{1,2},{2,3},{3,4},{4,5},{5,6},{6,7},{7,8},{8,9},{9,10},{10,1... | collective-permute-start | bytes 4718600 | tf_op jit(solution)/shard_map/ppermute | solution.py:14
  7.0 1.3 collective-permute-start.1
  8.3 1.5 copy.126
  10.4 25.3 %collective-permute-done = bf16[1,24,2,128,128]{3,4,1,2,0:T(8,128)(2,1)} collective-permute-done((bf16[1,24,2,128,128]{3,4,1,2,0:T(8,128)(2,1)S(1)}, bf16[1,24,2,128,128]{3,4,1,2,0:T(8,128)(2,1)}, u32[]{:S(2)}, u32[]{:S(2)}) %collective-permute-start) | collective-permute-done | bytes 1572896 | tf_op jit(solution)/shard_map/ppermute | solution.py:14
  35.7 5.1 %collective-permute-done.1 = bf16[1,24,2,128,128]{3,4,1,2,0:T(8,128)(2,1)} collective-permute-done((bf16[1,24,2,128,128]{3,4,1,2,0:T(8,128)(2,1)S(1)}, bf16[1,24,2,128,128]{3,4,1,2,0:T(8,128)(2,1)}, u32[]{:S(2)}, u32[]{:S(2)}) %collective-permute-start.1) | collective-permute-done | bytes 1572896 | tf_op jit(solution)/shard_map/ppermute | solution.py:15
  40.8 2.7 %fusion = bf16[24,2,128,128]{2,3,0,1:T(8,128)(2,1)S(1)} fusion(bf16[1,24,2,128,128]{3,4,1,2,0:T(8,128)(2,1)} %collective-permute-done.1, bf16[1,24,2,128,128]{3,4,1,2,0:T(8,128)(2,1)} %collective-permute-done, bf16[1,24,2,128,128]{3,4,1,2,0:T(8,128)(2,1)S(1)} %copy.48), kind=kLoop, calls=%fused_computation.5 | loop fusion | flops 5505024 | bytes 6291456 | tf_op jit(solution)/shard_map/add | solution.py:43
  43.5 0.7 fusion.30
  44.8 0.7 subtract_convert_fusion.1
  45.5 0.7 fusion.33
  46.2 0.7 add_convert_fusion.6
  46.9 0.7 fusion.32
  47.6 0.7 fusion.3
  48.3 0.7 fusion.4
  49.2 2.2 %gather_fusion = bf16[32,2,128,128]{3,2,1,0:T(8,128)(2,1)} fusion(bf16[24,2,128,128]{3,2,0,1:T(8,128)(2,1)S(1)} %pad_maximum_fusion.1, s32[1024]{0:T(1024)S(1)} %pad_clamp_fusion.1), kind=kCustom, calls=%fused_computation | custom fusion | bytes 4194432 | tf_op jit(solution)/shard_map/jit(_take)/gather | solution.py:90
  51.4 3.2 %broadcast_select_fusion = bf16[32,2,128,128]{3,2,1,0:T(8,128)(2,1)} fusion(bf16[32,2,128,128]{3,2,1,0:T(8,128)(2,1)} %gather_fusion, pred[32]{0:T(512)(128)(4,1)S(1)} %compare_and_fusion), kind=kLoop, calls=%fused_computation.4 | loop fusion | flops 1048576 | bytes 4194336 | tf_op jit(solution)/shard_map/jit(_take)/select_n | solution.py:90
  54.6 20.3 %all-to-all-start = ((bf16[32,2,128,128]{3,2,1,0:T(8,128)(2,1)}), bf16[32,2,128,128]{3,2,1,0:T(8,128)(2,1)S(1)}, u32[]{:S(2)}, u32[]{:S(2)}) async-start(bf16[32,2,128,128]{3,2,1,0:T(8,128)(2,1)} %broadcast_select_fusion), calls=%async_computation | async-start | bytes 4194304 | tf_op jit(solution)/shard_map/all_to_all | solution.py:91
  75.0 98.5 %all-to-all-done = bf16[32,2,128,128]{3,2,1,0:T(8,128)(2,1)S(1)} async-done(((bf16[32,2,128,128]{3,2,1,0:T(8,128)(2,1)}), bf16[32,2,128,128]{3,2,1,0:T(8,128)(2,1)S(1)}, u32[]{:S(2)}, u32[]{:S(2)}) %all-to-all-start) | async-done | bytes 2097184 | tf_op jit(solution)/shard_map/all_to_all | solution.py:91
  173.5 0.7 gather_fusion.1
  174.4 3.1 %collective-permute-start.2 = (bf16[12,2,128,128]{3,2,1,0:T(8,128)(2,1)S(1)}, bf16[12,2,128,128]{3,2,1,0:T(8,128)(2,1)S(1)}, u32[]{:S(2)}, u32[]{:S(2)}) collective-permute-start(bf16[12,2,128,128]{3,2,1,0:T(8,128)(2,1)S(1)} %broadcast_select_fusion.1), channel_id=1, source_target_pairs={{0,16},{16,32},{32,48},{48,64},{64,80},{80,96},{96,112},{112,128},... | collective-permute-start | bytes 2359304 | tf_op jit(solution)/shard_map/ppermute | solution.py:14
  177.4 0.7 fusion.121
  188.5 0.7 fusion.120
  192.0 4.6 %add_convert_fusion.1 = (bf16[12,2,128,128]{3,2,1,0:T(8,128)(2,1)S(1)}, bf16[12,2,128,128]{3,2,1,0:T(8,128)(2,1)S(1)}, bf16[12,2,128,128]{3,2,1,0:T(8,128)(2,1)S(1)}, bf16[12,2,128,128]{3,2,1,0:T(8,128)(2,1)S(1)}) fusion(bf16[36,2,128,128]{3,2,1,0:T(8,128)(2,1)S(1)} %pad_maximum_fusion, s32[]{:T(128)S(6)} %select_n.94, f32[]{:T(128)} %bitcast.61, ...), kind=kLoop, calls=%fused_computation.11 | loop fusion | flops 9437184 | bytes 9437248 | tf_op jit(solution)/shard_map/convert_element_type | solution.py:104
  206.8 1.2 copy.88
  (58 shorter events, 11.8 us)
Async XLA Ops:
  1.9 33.8 %collective-permute-start = (bf16[1,24,2,128,128]{3,4,1,2,0:T(8,128)(2,1)S(1)}, bf16[1,24,2,128,128]{3,4,1,2,0:T(8,128)(2,1)}, u32[]{:S(2)}, u32[]{:S(2)}) collective-permute-start(bf16[1,24,2,128,128]{3,4,1,2,0:T(8,128)(2,1)S(1)} %copy.48), channel_id=1, source_target_pairs={{0,1},{1,2},{2,3},{3,4},{4,5},{5,6},{6,7},{7,8},{8,9},{9,10},{10,1... | collective-permute-start | bytes 4718600 | tf_op jit(solution)/shard_map/ppermute | solution.py:14
  7.0 33.7 %collective-permute-start.1 = (bf16[1,24,2,128,128]{3,4,1,2,0:T(8,128)(2,1)S(1)}, bf16[1,24,2,128,128]{3,4,1,2,0:T(8,128)(2,1)}, u32[]{:S(2)}, u32[]{:S(2)}) collective-permute-start(bf16[1,24,2,128,128]{3,4,1,2,0:T(8,128)(2,1)S(1)} %copy.48), channel_id=1, source_target_pairs={{1,0},{2,1},{3,2},{4,3},{5,4},{6,5},{7,6},{8,7},{9,8},{10,9},{11,1... | collective-permute-start | bytes 4718600 | tf_op jit(solution)/shard_map/ppermute | solution.py:15
  8.3 1.6 copy-start.1
  54.6 118.9 %all-to-all-start = ((bf16[32,2,128,128]{3,2,1,0:T(8,128)(2,1)}), bf16[32,2,128,128]{3,2,1,0:T(8,128)(2,1)S(1)}, u32[]{:S(2)}, u32[]{:S(2)}) async-start(bf16[32,2,128,128]{3,2,1,0:T(8,128)(2,1)} %broadcast_select_fusion), calls=%async_computation | async-start | bytes 4194304 | tf_op jit(solution)/shard_map/all_to_all | solution.py:91
  75.0 102.5 %copy-start.2 = (s32[4]{0:T(128)S(1)}, s32[4]{0:T(128)}, u32[]{:S(2)}) copy-start(s32[4]{0:T(128)} %param.11) | copy-start | bytes 52
  75.0 113.5 %copy-start.3 = (f32[4]{0:T(128)S(1)}, f32[4]{0:T(128)}, u32[]{:S(2)}) copy-start(f32[4]{0:T(128)} %param.9) | copy-start | bytes 52
  174.4 17.4 %collective-permute-start.2 = (bf16[12,2,128,128]{3,2,1,0:T(8,128)(2,1)S(1)}, bf16[12,2,128,128]{3,2,1,0:T(8,128)(2,1)S(1)}, u32[]{:S(2)}, u32[]{:S(2)}) collective-permute-start(bf16[12,2,128,128]{3,2,1,0:T(8,128)(2,1)S(1)} %broadcast_select_fusion.1), channel_id=1, source_target_pairs={{0,16},{16,32},{32,48},{48,64},{64,80},{80,96},{96,112},{112,128},... | collective-permute-start | bytes 2359304 | tf_op jit(solution)/shard_map/ppermute | solution.py:14
  177.4 14.3 %collective-permute-start.3 = (bf16[12,2,128,128]{3,2,1,0:T(8,128)(2,1)S(1)}, bf16[12,2,128,128]{3,2,1,0:T(8,128)(2,1)S(1)}, u32[]{:S(2)}, u32[]{:S(2)}) collective-permute-start(bf16[12,2,128,128]{3,2,1,0:T(8,128)(2,1)S(1)} %broadcast_select_fusion.1), channel_id=1, source_target_pairs={{16,0},{32,16},{48,32},{64,48},{80,64},{96,80},{112,96},{128,112},... | collective-permute-start | bytes 2359304 | tf_op jit(solution)/shard_map/ppermute | solution.py:15
  192.0 4.6 %copy-start = (bf16[4,2,128,128]{3,2,1,0:T(8,128)(2,1)S(1)}, bf16[4,2,128,128]{3,2,1,0:T(8,128)(2,1)}, u32[]{:S(2)}) copy-start(bf16[4,2,128,128]{3,2,1,0:T(8,128)(2,1)} %param.8) | copy-start | bytes 786436
where the time goes:
time: 209 us; the launch traced here: 208 us
  waiting for transfers between devices  129 us (62%)
  starting transfers between devices  29.8 us (14%)
  matrix products  15 us (7%)
  between operations  13.4 us (6%)
  other arithmetic  12.1 us (6%)
  local copies, waits for them, and re-layouts  8.92 us (4%)
    all_to_all x1, waiting for transfers between devices, body(): lax.all_to_all(outgoing, 'energy', split_axis=0, concat_axis=0, tiled=True)  98.5 us
    ppermute x2, waiting for transfers between devices, with_halo(): before = lax.ppermute(last, axis, up)  25.3 us
    all_to_all x1, starting transfers between devices, body(): lax.all_to_all(outgoing, 'energy', split_axis=0, concat_axis=0, tiled=True)  20.3 us
    ppermute x2, starting transfers between devices, with_halo(): before = lax.ppermute(last, axis, up)  8.17 us
    ppermute x2, waiting for transfers between devices, with_halo(): after = lax.ppermute(initial, axis, down)  5.09 us
    convert_element_type x1, other arithmetic, body(): ((weight_one + 1.0) * shifted_up + weight_one * shifted_down).astype(jnp....  4.57 us
  transfers between devices with their start and end apart: 5, of which 3 were waited for; matrix products, arithmetic and copies ran while one was open for 2% of the time, Pallas kernels for 0%

commit v1 on v0

--- a/solution.py
+++ b/solution.py
@@ -1,7 +1,19 @@
+import functools
+
 import jax
 import jax.numpy as jnp
 from jax import lax
+from jax.experimental import pallas as pl
+from jax.experimental.pallas import tpu as pltpu
 from jax.sharding import PartitionSpec as P
+
+MESH = pl.DeviceIdType.MESH
+LAG = 5
+START = 3
+PLAG = 3
+AHEAD = 6
+STEPS = 112
+SIZES = (88, 104)
 
 
 def with_halo(array, sides, width, wrap):
@@ -63,7 +75,7 @@
     return jnp.stack([out_real, out_imag], 1)
 
 
-def body(retarded, self_lesser, coupling, occupancy, adaptive_owner, phonon_offsets):
+def general(retarded, self_lesser, coupling, occupancy, adaptive_owner, phonon_offsets):
     n_energy = lax.axis_size("energy")
     my_index = lax.axis_index("energy")
     energies = adaptive_owner.shape[0]
@@ -108,6 +120,408 @@
     return accumulated[None]
 
 
+def packets(owner):
+    e = jnp.arange(384, dtype=jnp.int32)
+    chip, upper = owner // 2, (e // 12) % 2 == 1
+    d = (e // 24 - chip + 16) % 16
+    plus = jnp.where(upper, d <= 7, (d >= 1) & (d <= 8))
+    there = jnp.where(upper, d + 1, d)
+    back = jnp.where(upper, 16 - d, jnp.where(d == 0, 1, 17 - d))
+    reach = jnp.where(plus, there, back)
+    way = jnp.where(plus, 0, 1)
+    stop = jnp.where(plus, chip, (16 - chip) % 16)
+    train = way * 16 + stop
+    key = (8 - reach) * 384 + e
+    same = owner[:, None] == owner[None, :]
+    before = key[None, :] < key[:, None]
+    rank = jnp.sum((same & before).astype(jnp.int32), axis=1)
+    slot = jnp.sum((same & (e[None, :] < e[:, None])).astype(jnp.int32), axis=1)
+    place = jnp.sum(((train[:, None] == train[None, :]) & before).astype(jnp.int32), axis=1)
+    return way, stop, train, reach, rank, slot, place
+
+
+def counts(train, reach, rank, place):
+    lane = jnp.arange(128, dtype=jnp.int32)
+    hops = jnp.arange(8, dtype=jnp.int32)
+    source = (lane // 16) * 16 + (lane[None, :] - hops[:, None] + 16) % 16
+    through = (source[:, :, None] == train[None, None, :]) & (reach[None, None, :] > hops[:, None, None])
+    passing = jnp.sum(through.astype(jnp.int32), axis=2)
+    ready = jnp.arange(32, dtype=jnp.int32)
+    held = (lane[None, :, None] == train[None, None, :]) & (rank[None, None, :] >= ready[:, None, None])
+    first = jnp.min(jnp.where(held, place[None, None, :], 384), axis=2)
+    return passing, jnp.minimum(first, passing[:1])
+
+
+def schedule_kernel(passing_ref, ready_ref, code_ref, sent_ref):
+    lane = lax.broadcasted_iota(jnp.int32, (1, 128), 1)
+    edge = lane % 16 == 0
+    limit = [passing_ref[i : i + 1, :] for i in range(8)]
+    zero = jnp.zeros((1, 128), jnp.int32)
+    for t in range(LAG):
+        sent_ref[t] = jnp.zeros((8, 128), jnp.int32)
+
+    def slot(t, sent):
+        ready = jnp.clip((t - START + 2) // 2, 0, 24)
+        code = zero - 1
+        taken = lane < 0
+        out = []
+        for i in range(8):
+            if i == 0:
+                there = ready_ref[pl.ds(ready, 1), :]
+            else:
+                old = sent_ref[t, i - 1 : i, :]
+                there = jnp.where(edge, pltpu.roll(old, 113, 1), pltpu.roll(old, 1, 1))
+                there = jnp.minimum(there, limit[i])
+            go = (sent[i] < there) & ~taken
+            code = jnp.where(go, sent[i] + 64 * i, code)
+            taken = taken | go
+            out.append(jnp.where(go, sent[i] + 1, sent[i]))
+            sent_ref[t + LAG, i : i + 1, :] = out[i]
+        code_ref[pl.ds(t, 1), :] = code
+        return tuple(out)
+
+    lax.fori_loop(0, STEPS, slot, (zero,) * 8)
+
+
+def schedule(passing, ready):
+    return pl.pallas_call(
+        schedule_kernel,
+        out_shape=jax.ShapeDtypeStruct((STEPS, 128), jnp.int32),
+        in_specs=[pl.BlockSpec(memory_space=pltpu.VMEM)] * 2,
+        out_specs=pl.BlockSpec(memory_space=pltpu.VMEM),
+        scratch_shapes=[pltpu.VMEM((STEPS + LAG, 8, 128), jnp.int32)],
+    )(passing, ready)
+
+
+def tables(owner, offsets, me):
+    way, stop, train, reach, rank, slot, place = packets(owner)
+    passing, ready = counts(train, reach, rank, place)
+    code = schedule(passing, ready)
+    used = code[:, :32] >= 0
+    steps = jnp.arange(STEPS, dtype=jnp.int32)
+    whole = jnp.sum(used.astype(jnp.int32)) == jnp.sum(passing[:, :32])
+    needed = jnp.max(jnp.where(used, steps[:, None] + 1, 0))
+    needed = jnp.where(whole, needed, STEPS + 1)
+    chip, core = me // 2, me % 2
+
+    def lane_of(way_index, back):
+        at = jnp.where(way_index == 0, chip, (16 - chip) % 16)
+        return way_index * 16 + (at - back + 16) % 16
+
+    def column(index):
+        return lax.dynamic_slice_in_dim(code, index, 1, 1)[:, 0]
+
+    leaving = column(lane_of(core, 0))
+    arriving = column(lane_of(core, 1))
+    other = column(lane_of(1 - core, 1))
+    at = jnp.where(way == 0, chip, (16 - chip) % 16)
+    hops = (at - stop + 16) % 16
+    mine = way == core
+    local = jnp.where(owner % 2 == core, rank, 24 + rank)
+    came = (hops - 1) * 64 + place
+    lanes = jnp.where(mine[:, None], arriving[None, :], other[None, :])
+    stored = jnp.sum(jnp.where(lanes == came[:, None], steps[None, :], 0), axis=1)
+    where = jnp.where(hops == 0, local, 48 + 2 * stored + jnp.where(mine, 0, 1))
+    passed = mine & (hops < reach)
+    goes = jnp.where(passed, hops * 64 + place, -2)
+    index = jnp.sum(jnp.where(leaving[:, None] == goes[None, :], where[None, :], 0), axis=1)
+    own = owner == me
+    ranks = jnp.arange(24, dtype=jnp.int32)
+    order = jnp.sum(jnp.where(own[None, :] & (rank[None, :] == ranks[:, None]), slot[None, :], 0), axis=1)
+    around = jnp.concatenate([where[-12:], where, where[:12]])
+    location = lax.dynamic_slice_in_dim(around, me * 12, 36)
+    table = jnp.concatenate([index, order, location, offsets])
+    return table, needed
+
+
+def wide(real, imag):
+    return jnp.concatenate([real, imag], axis=1)
+
+
+def main_kernel(
+    size,
+    table,
+    weights,
+    ret_hbm,
+    sig_hbm,
+    coupling_ref,
+    out_ref,
+    ret,
+    sig,
+    outgoing,
+    lower,
+    upper,
+    twin,
+    landed,
+    relayed,
+    sending,
+    pool,
+    left_mats,
+    right_mats,
+    load_sem,
+    low_send,
+    up_send,
+    low_recv,
+    up_recv,
+    twin_send,
+    twin_recv,
+    ring_send,
+    ring_recv,
+    relay_send,
+    relay_recv,
+):
+    at_order, at_location, at_offset = STEPS, STEPS + 24, STEPS + 60
+    energy, slab = lax.axis_index("energy"), lax.axis_index("slab")
+    core = lax.rem(energy, 2)
+    step = 2 - 4 * core
+    ahead = (lax.rem(energy + step + 32, 32), slab)
+    behind = (lax.rem(energy - step + 32, 32), slab)
+    partner = (energy + 1 - 2 * core, slab)
+    slab_up = (energy, lax.rem(slab + 1, 16))
+    slab_down = (energy, lax.rem(slab + 15, 16))
+    has_lower = jnp.where(slab > 0, 0.5, 0.0)
+    has_upper = jnp.where(slab < 15, 0.5, 0.0)
+
+    load_sig = pltpu.make_async_copy(sig_hbm.at[0], sig, load_sem.at[0])
+    load_ret = pltpu.make_async_copy(ret_hbm.at[0], ret, load_sem.at[1])
+    load_sig.start()
+    load_ret.start()
+
+    barrier = pltpu.get_barrier_semaphore()
+    for device in (ahead, behind, partner, slab_up, slab_down):
+        pl.semaphore_signal(barrier, inc=1, device_id=device, device_id_type=MESH)
+
+    def remote(source, target, send, receive, device):
+        return pltpu.make_async_remote_copy(
+            src_ref=source,
+            dst_ref=target,
+            send_sem=send,
+            recv_sem=receive,
+            device_id=device,
+            device_id_type=MESH,
+        )
+
+    def to_upper(j):
+        return remote(outgoing.at[j], lower.at[j], up_send.at[j], low_recv.at[j], slab_up)
+
+    def to_lower(j):
+        return remote(outgoing.at[j], upper.at[j], low_send.at[j], up_recv.at[j], slab_down)
+
+    def to_twin(j):
+        return remote(pool.at[j], twin.at[j], twin_send.at[j], twin_recv.at[j], partner)
+
+    def to_ring(t):
+        return remote(sending.at[t], landed.at[t], ring_send.at[t], ring_recv.at[t], ahead)
+
+    def to_relay(t):
+        return remote(landed.at[t], relayed.at[t], relay_send.at[t], relay_recv.at[t], partner)
+
+    def spread(j):
+        outgoing[j] = sig[table[at_order + j]]
+        to_upper(j).start()
+        to_lower(j).start()
+
+    load_sig.wait()
+    pl.semaphore_wait(barrier, 5)
+    for j in range(AHEAD):
+        spread(j)
+    for k in range(4):
+        m_real, m_imag = coupling_ref[k, 0], coupling_ref[k, 1]
+        left_mats[k] = jnp.concatenate([wide(m_real, -m_imag), wide(m_imag, m_real)], axis=0)
+        right_mats[:, 256 * k : 256 * k + 256] = jnp.concatenate(
+            [wide(m_real, m_imag), wide(-m_imag, m_real)], axis=0
+        )
+    load_ret.wait()
+
+    def form(j):
+        to_upper(j).wait_recv()
+        to_lower(j).wait_recv()
+        beside = lower[j].astype(jnp.float32) * has_lower + upper[j].astype(jnp.float32) * has_upper
+        total = (outgoing[j].astype(jnp.float32) + beside).astype(jnp.bfloat16)
+        s_real, s_imag = total[0], total[1]
+        block = ret[table[at_order + j]]
+        r_real, r_imag = block[0], block[1]
+        right = jnp.concatenate([wide(s_real, s_imag), wide(-s_imag, s_real)], axis=0)
+        half = jnp.dot(wide(r_real, r_imag), right, preferred_element_type=jnp.float32).astype(jnp.bfloat16)
+        back = jnp.concatenate([wide(r_real, r_imag), wide(-r_imag, r_real)], axis=0)
+        full = lax.dot_general(half, back, (((1,), (1,)), ((), ())), preferred_element_type=jnp.float32)
+        full = full.astype(jnp.bfloat16)
+        pool[j, 0] = full[:, :128]
+        pool[j, 1] = full[:, 128:]
+        to_twin(j).start()
+
+    def take_twin(j):
+        to_twin(j).wait_recv()
+        pool[24 + j] = twin[j]
+
+    def take_ring(t):
+        to_ring(t).wait_recv()
+        to_relay(t).start()
+        pool[48 + 2 * t] = landed[t]
+
+    def take_relay(t):
+        to_relay(t).wait_recv()
+        pool[49 + 2 * t] = relayed[t]
+
+    def send_ring(t):
+        sending[t] = pool[table[t]]
+        to_ring(t).start()
+
+    def early(j, carry):
+        @pl.when(j < 24 - AHEAD)
+        def _():
+            spread(j + AHEAD)
+
+        form(j)
+
+        @pl.when(j >= 1)
+        def _():
+            take_twin(j - 1)
+
+        for half in (0, 1):
+            t = 2 * j + half
+
+            @pl.when(t >= LAG)
+            def _():
+                take_ring(t - LAG)
+
+            send_ring(t)
+
+            @pl.when(t >= LAG + PLAG)
+            def _():
+                take_relay(t - LAG - PLAG)
+
+        return carry
+
+    lax.fori_loop(0, 24, early, 0)
+    take_twin(23)
+
+    def late(t, carry):
+        take_ring(t - LAG)
+        send_ring(t)
+        take_relay(t - LAG - PLAG)
+        return carry
+
+    lax.fori_loop(48, size, late, 0)
+
+    def last(t, carry):
+        take_ring(t)
+        return carry
+
+    lax.fori_loop(size - LAG, size, last, 0)
+
+    def final(t, carry):
+        take_relay(t)
+        return carry
+
+    lax.fori_loop(size - LAG - PLAG, size, final, 0)
+
+    def weighted(i, k):
+        offset = table[at_offset + k]
+        up = pool[table[at_location + 12 + i + offset]].astype(jnp.float32)
+        down = pool[table[at_location + 12 + i - offset]].astype(jnp.float32)
+        value = (weights[k] + 1.0) * up + weights[k] * down
+        return value.astype(jnp.bfloat16).reshape(256, 128)
+
+    def finish(p, carry):
+        coupled = []
+        for k in range(4):
+            pair = wide(weighted(2 * p, k), weighted(2 * p + 1, k))
+            left = jnp.dot(left_mats[k], pair, preferred_element_type=jnp.float32).astype(jnp.bfloat16)
+            rows = [wide(left[:128, c : c + 128], left[128:, c : c + 128]) for c in (0, 128)]
+            coupled.append(jnp.concatenate(rows, axis=0))
+        whole = jnp.concatenate(coupled, axis=1)
+        result = lax.dot_general(
+            whole, right_mats[...], (((1,), (1,)), ((), ())), preferred_element_type=jnp.float32
+        )
+        for c in (0, 1):
+            out_ref[0, 2 * p + c, 0] = result[128 * c : 128 * c + 128, :128]
+            out_ref[0, 2 * p + c, 1] = result[128 * c : 128 * c + 128, 128:]
+        return carry
+
+    lax.fori_loop(0, 6, finish, 0)
+
+    def drain_x(j, carry):
+        to_upper(j).wait_send()
+        to_lower(j).wait_send()
+        to_twin(j).wait_send()
+        return carry
+
+    lax.fori_loop(0, 24, drain_x, 0)
+
+    def drain_z(t, carry):
+        to_ring(t).wait_send()
+        to_relay(t).wait_send()
+        return carry
+
+    lax.fori_loop(0, size, drain_z, 0)
+
+
+def routed(size, identity, table, occupancy, retarded, self_lesser, coupling):
+    def blocks(n):
+        return pltpu.VMEM((n, 2, 128, 128), jnp.bfloat16)
+
+    dma = pltpu.SemaphoreType.DMA
+    return pl.pallas_call(
+        functools.partial(main_kernel, size),
+        out_shape=jax.ShapeDtypeStruct((1, 12, 2, 128, 128), jnp.float32),
+        in_specs=[
+            pl.BlockSpec(memory_space=pltpu.SMEM),
+            pl.BlockSpec(memory_space=pltpu.SMEM),
+            pl.BlockSpec(memory_space=pl.ANY),
+            pl.BlockSpec(memory_space=pl.ANY),
+            pl.BlockSpec(memory_space=pltpu.VMEM),
+        ],
+        out_specs=pl.BlockSpec(memory_space=pltpu.VMEM),
+        scratch_shapes=[
+            blocks(24),
+            blocks(24),
+            blocks(24),
+            blocks(24),
+            blocks(24),
+            blocks(24),
+            blocks(size),
+            blocks(size),
+            blocks(size),
+            blocks(48 + 2 * size),
+            pltpu.VMEM((4, 256, 256), jnp.bfloat16),
+            pltpu.VMEM((256, 1024), jnp.bfloat16),
+            dma((2,)),
+            dma((24,)),
+            dma((24,)),
+            dma((24,)),
+            dma((24,)),
+            dma((24,)),
+            dma((24,)),
+            dma((size,)),
+            dma((size,)),
+            dma((size,)),
+            dma((size,)),
+        ],
+        compiler_params=pltpu.CompilerParams(
+            collective_id=identity, has_side_effects=True, vmem_limit_bytes=60 * 1024 * 1024
+        ),
+    )(table, occupancy, retarded, self_lesser, coupling)
+
+
+def body(retarded, self_lesser, coupling, occupancy, adaptive_owner, phonon_offsets):
+    me = lax.axis_index("energy")
+    table, needed = tables(adaptive_owner, phonon_offsets, me)
+    choice = sum((needed > size).astype(jnp.int32) for size in SIZES)
+
+    def fast(size, identity):
+        def call(_):
+            return routed(size, identity, table, occupancy, retarded, self_lesser, coupling)
+
+        return call
+
+    def slow(_):
+        return general(retarded, self_lesser, coupling, occupancy, adaptive_owner, phonon_offsets)
+
+    branches = [fast(size, i) for i, size in enumerate(SIZES)] + [slow]
+    return lax.switch(choice, branches, 0)
+
+
 def solution(mesh):
     placed = (
         P("slab", "energy", None, None, None),

time: 209 us -> 235 us (1.12)
  loops' own time: 0 us -> 13.3 us
  between operations: 13.4 us -> 2.08 us
  Pallas kernels: 0 us -> 10.9 us
  other arithmetic: 12.1 us -> 22.5 us
    another operation x0 -> x1, loops' own time: none -> 13.3 us  [body(): return lax.switch(choice, branches, 0)]
    pallas_call x0 -> x1, Pallas kernels: none -> 10.9 us  [schedule(): pl.pallas_call(schedule_kernel, out_shape=jax.ShapeDtypeStruct((STEPS, 12...]
    reduce_sum x2 -> x8, other arithmetic: 0.43 us -> 3.97 us  [the longest x1 1.37 us: packets(): slot = jnp.sum((same & (e[None, :] < e[:, None])).astype(jnp.int32), axis=1)]
    another operation x0 -> x2, local copies, waits for them, and re-layouts: none -> 2.88 us
    select_n x4 -> x7, other arithmetic: 3.35 us -> 4.77 us  [the longest x2 3.2 us: general(): outgoing = jnp.take(formed, send_slot, axis=0)]
  transfers between devices with their start and end apart: 5 -> 5, of which waited for: 3 -> 3; matrix products, arithmetic and copies ran while one was open for 2% -> 1% of each run, Pallas kernels for 0% -> 0%
where the time goes in v1:
time: 235 us; the launch traced here: 234 us
  waiting for transfers between devices  130 us (55%)
  starting transfers between devices  29.9 us (13%)
  other arithmetic  22.5 us (10%)
  matrix products  15 us (6%)
  loops' own time  13.3 us (6%)
  Pallas kernels  10.9 us (5%)
  local copies, waits for them, and re-layouts  10.1 us (4%)
    all_to_all x1, waiting for transfers between devices, general(): lax.all_to_all(outgoing, 'energy', split_axis=0, concat_axis=0, tiled=True)  98.6 us
    ppermute x2, waiting for transfers between devices, with_halo(): before = lax.ppermute(last, axis, up)  26.3 us
    all_to_all x1, starting transfers between devices, general(): lax.all_to_all(outgoing, 'energy', split_axis=0, concat_axis=0, tiled=True)  20.3 us
    another operation x1, loops' own time, body(): return lax.switch(choice, branches, 0)  13.3 us
    pallas_call x1, Pallas kernels, schedule(): pl.pallas_call(schedule_kernel, out_shape=jax.ShapeDtypeStruct((STEPS, 12...  10.9 us
    ppermute x2, starting transfers between devices, with_halo(): before = lax.ppermute(last, axis, up)  8.1 us
    ppermute x2, waiting for transfers between devices, with_halo(): after = lax.ppermute(initial, axis, down)  4.97 us
  transfers between devices with their start and end apart: 5, of which 3 were waited for; matrix products, arithmetic and copies ran while one was open for 1% of the time, Pallas kernels for 0%

profile of v1, /device:TPU:1, one launch (start us, length us, event | category | flops | bytes accessed | tf_op | source)
XLA Modules:
  0.0 233.6 jit_solution(14306273763678242013)
XLA Ops:
  0.0 0.7 add_select_fusion.7
  0.7 1.4 convert_reduce_fusion.3
  2.2 1.1 select_reduce_fusion.1
  4.5 10.9 %shard_map.67 = s32[112,128]{1,0:T(8,128)} custom-call(s32[8,128]{1,0:T(8,128)} %copy-done.3, s32[32,128]{1,0:T(8,128)} %broadcast_minimum_fusion.ready_ref), custom_call_target="tpu_custom_call" | custom-call | tf_op jit(solution)/shard_map/pallas_call | solution.py:187
  15.4 1.2 dynamic-slice_reduce_fusion.2
  18.6 0.7 pad_add_fusion.1
  19.3 1.6 select_reduce_fusion.4
  21.0 1.3 slice_reduce_fusion
  24.3 208.2 %conditional.1 = (f32[1,12,2,128,128]{4,3,2,1,0:T(8,128)S(1)}) conditional(s32[]{:T(128)} %clamp.3, (s32[176]{0:T(256)S(1)}, f32[4]{0:T(128)}, bf16[1,24,2,128,128]{4,3,2,1,0:T(8,128)(2,1)}, bf16[1,24,2,128,128]{4,3,2,1,0:T(8,128)(2,1)}, bf16[4,2,128,128]{3,2,1,0:T(8,128)(2,1)}) %tuple.14, (s32[176]{0:T(256)S(1)}, f32[4]{0:T(128)}, ...), branch_computations={%region_11.12_spmd, %region_12.13_spmd, %region_13.17_spmd} | conditional | flops 2447450624 | bytes 161513376 | solution.py:522
  24.3 2.7 %copy.130 = bf16[1,24,2,128,128]{3,4,1,2,0:T(8,128)(2,1)} copy(bf16[1,24,2,128,128]{4,3,2,1,0:T(8,128)(2,1)} %get-tuple-element.78) | data formatting | bytes 3145728 | tf_op jit(solution)/shard_map
  27.0 5.1 %collective-permute-start = (bf16[1,24,2,128,128]{3,4,1,2,0:T(8,128)(2,1)}, bf16[1,24,2,128,128]{3,4,1,2,0:T(8,128)(2,1)}, u32[]{:S(2)}, u32[]{:S(2)}) collective-permute-start(bf16[1,24,2,128,128]{3,4,1,2,0:T(8,128)(2,1)} %copy.130), channel_id=1, source_target_pairs={{0,1},{1,2},{2,3},{3,4},{4,5},{5,6},{6,7},{7,8},{8,9},{9,10},{10,1... | collective-permute-start | bytes 4718600 | tf_op jit(solution)/shard_map/cond/branch_2_fun/ppermute | solution.py:26
  32.1 1.5 collective-permute-start.1
  34.7 26.3 %collective-permute-done = bf16[1,24,2,128,128]{3,4,1,2,0:T(8,128)(2,1)} collective-permute-done((bf16[1,24,2,128,128]{3,4,1,2,0:T(8,128)(2,1)}, bf16[1,24,2,128,128]{3,4,1,2,0:T(8,128)(2,1)}, u32[]{:S(2)}, u32[]{:S(2)}) %collective-permute-start) | collective-permute-done | bytes 1572896 | tf_op jit(solution)/shard_map/cond/branch_2_fun/ppermute | solution.py:26
  61.1 5.0 %collective-permute-done.1 = bf16[1,24,2,128,128]{3,4,1,2,0:T(8,128)(2,1)} collective-permute-done((bf16[1,24,2,128,128]{3,4,1,2,0:T(8,128)(2,1)}, bf16[1,24,2,128,128]{3,4,1,2,0:T(8,128)(2,1)}, u32[]{:S(2)}, u32[]{:S(2)}) %collective-permute-start.1) | collective-permute-done | bytes 1572896 | tf_op jit(solution)/shard_map/cond/branch_2_fun/ppermute | solution.py:27
  66.0 3.2 %fusion = bf16[24,2,128,128]{2,3,0,1:T(8,128)(2,1)S(1)} fusion(bf16[1,24,2,128,128]{3,4,1,2,0:T(8,128)(2,1)} %collective-permute-done.1, bf16[1,24,2,128,128]{3,4,1,2,0:T(8,128)(2,1)} %collective-permute-done, bf16[1,24,2,128,128]{3,4,1,2,0:T(8,128)(2,1)} %copy.130), kind=kLoop, calls=%fused_computation.5 | loop fusion | flops 5505024 | bytes 6291456 | tf_op jit(solution)/shard_map/cond/branch_2_fun/add | solution.py:55
  71.3 0.7 fusion.33
  72.7 0.7 fusion.32
  74.9 2.2 gather_fusion
  77.1 3.2 %broadcast_select_fusion = bf16[32,2,128,128]{3,2,1,0:T(8,128)(2,1)} fusion(bf16[32,2,128,128]{3,2,1,0:T(8,128)(2,1)} %gather_fusion, pred[32]{0:T(512)(128)(4,1)S(1)} %compare_and_fusion), kind=kLoop, calls=%fused_computation.4 | loop fusion | flops 1048576 | bytes 4194336 | tf_op jit(solution)/shard_map/cond/branch_2_fun/jit(_take)/select_n | solution.py:102
  80.3 20.3 %all-to-all-start = ((bf16[32,2,128,128]{3,2,1,0:T(8,128)(2,1)}), bf16[32,2,128,128]{3,2,1,0:T(8,128)(2,1)S(1)}, u32[]{:S(2)}, u32[]{:S(2)}) async-start(bf16[32,2,128,128]{3,2,1,0:T(8,128)(2,1)} %broadcast_select_fusion), calls=%async_computation | async-start | bytes 4194304 | tf_op jit(solution)/shard_map/cond/branch_2_fun/all_to_all | solution.py:103
  100.7 98.6 %all-to-all-done = bf16[32,2,128,128]{3,2,1,0:T(8,128)(2,1)S(1)} async-done(((bf16[32,2,128,128]{3,2,1,0:T(8,128)(2,1)}), bf16[32,2,128,128]{3,2,1,0:T(8,128)(2,1)S(1)}, u32[]{:S(2)}, u32[]{:S(2)}) %all-to-all-start) | async-done | bytes 2097184 | tf_op jit(solution)/shard_map/cond/branch_2_fun/all_to_all | solution.py:103
  200.1 3.0 %collective-permute-start.2 = (bf16[12,2,128,128]{3,2,1,0:T(8,128)(2,1)S(1)}, bf16[12,2,128,128]{3,2,1,0:T(8,128)(2,1)S(1)}, u32[]{:S(2)}, u32[]{:S(2)}) collective-permute-start(bf16[12,2,128,128]{3,2,1,0:T(8,128)(2,1)S(1)} %broadcast_select_fusion.1), channel_id=1, source_target_pairs={{0,16},{16,32},{32,48},{48,64},{64,80},{80,96},{96,112},{112,128},... | collective-permute-start | bytes 2359304 | tf_op jit(solution)/shard_map/cond/branch_2_fun/ppermute | solution.py:26
  217.3 4.5 %add_convert_fusion.1 = (bf16[12,2,128,128]{3,2,1,0:T(8,128)(2,1)S(1)}, bf16[12,2,128,128]{3,2,1,0:T(8,128)(2,1)S(1)}, bf16[12,2,128,128]{3,2,1,0:T(8,128)(2,1)S(1)}, bf16[12,2,128,128]{3,2,1,0:T(8,128)(2,1)S(1)}) fusion(bf16[36,2,128,128]{3,2,1,0:T(8,128)(2,1)S(1)} %pad_maximum_fusion, s32[]{:T(128)S(6)} %select_n.212, f32[]{:T(128)} %bitcast.61, ...), kind=kLoop, calls=%fused_computation.11 | loop fusion | flops 9437184 | bytes 9437248 | tf_op jit(solution)/shard_map/cond/branch_2_fun/convert_element_type | solution.py:116
  232.5 1.1 copy.178
  (93 shorter events, 21.2 us)
Async XLA Ops:
  3.8 0.6 copy-start.3
  24.3 9.3 %copy-start = (bf16[1,24,2,128,128]{4,3,2,1,0:T(8,128)(2,1)S(1)}, bf16[1,24,2,128,128]{4,3,2,1,0:T(8,128)(2,1)}, u32[]{:S(2)}) copy-start(bf16[1,24,2,128,128]{4,3,2,1,0:T(8,128)(2,1)} %get-tuple-element.79) | copy-start | bytes 4718596 | tf_op jit(solution)/shard_map/cond
  27.0 34.1 %collective-permute-start = (bf16[1,24,2,128,128]{3,4,1,2,0:T(8,128)(2,1)}, bf16[1,24,2,128,128]{3,4,1,2,0:T(8,128)(2,1)}, u32[]{:S(2)}, u32[]{:S(2)}) collective-permute-start(bf16[1,24,2,128,128]{3,4,1,2,0:T(8,128)(2,1)} %copy.130), channel_id=1, source_target_pairs={{0,1},{1,2},{2,3},{3,4},{4,5},{5,6},{6,7},{7,8},{8,9},{9,10},{10,1... | collective-permute-start | bytes 4718600 | tf_op jit(solution)/shard_map/cond/branch_2_fun/ppermute | solution.py:26
  32.1 34.0 %collective-permute-start.1 = (bf16[1,24,2,128,128]{3,4,1,2,0:T(8,128)(2,1)}, bf16[1,24,2,128,128]{3,4,1,2,0:T(8,128)(2,1)}, u32[]{:S(2)}, u32[]{:S(2)}) collective-permute-start(bf16[1,24,2,128,128]{3,4,1,2,0:T(8,128)(2,1)} %copy.130), channel_id=1, source_target_pairs={{1,0},{2,1},{3,2},{4,3},{5,4},{6,5},{7,6},{8,7},{9,8},{10,9},{11,1... | collective-permute-start | bytes 4718600 | tf_op jit(solution)/shard_map/cond/branch_2_fun/ppermute | solution.py:27
  33.6 0.7 copy-start.2
  80.3 119.0 %all-to-all-start = ((bf16[32,2,128,128]{3,2,1,0:T(8,128)(2,1)}), bf16[32,2,128,128]{3,2,1,0:T(8,128)(2,1)S(1)}, u32[]{:S(2)}, u32[]{:S(2)}) async-start(bf16[32,2,128,128]{3,2,1,0:T(8,128)(2,1)} %broadcast_select_fusion), calls=%async_computation | async-start | bytes 4194304 | tf_op jit(solution)/shard_map/cond/branch_2_fun/all_to_all | solution.py:103
  100.7 102.5 %copy-start.5 = (s32[4]{0:T(128)S(1)}, s32[4]{0:T(128)}, u32[]{:S(2)}) copy-start(s32[4]{0:T(128)} %get-tuple-element.55) | copy-start | bytes 52 | tf_op jit(solution)/shard_map/cond
  100.7 113.2 %copy-start.4 = (f32[4]{0:T(128)S(1)}, f32[4]{0:T(128)}, u32[]{:S(2)}) copy-start(f32[4]{0:T(128)} %get-tuple-element.51) | copy-start | bytes 52 | tf_op jit(solution)/shard_map/cond
  200.1 16.9 %collective-permute-start.2 = (bf16[12,2,128,128]{3,2,1,0:T(8,128)(2,1)S(1)}, bf16[12,2,128,128]{3,2,1,0:T(8,128)(2,1)S(1)}, u32[]{:S(2)}, u32[]{:S(2)}) collective-permute-start(bf16[12,2,128,128]{3,2,1,0:T(8,128)(2,1)S(1)} %broadcast_select_fusion.1), channel_id=1, source_target_pairs={{0,16},{16,32},{32,48},{48,64},{64,80},{80,96},{96,112},{112,128},... | collective-permute-start | bytes 2359304 | tf_op jit(solution)/shard_map/cond/branch_2_fun/ppermute | solution.py:26
  203.2 13.9 %collective-permute-start.3 = (bf16[12,2,128,128]{3,2,1,0:T(8,128)(2,1)S(1)}, bf16[12,2,128,128]{3,2,1,0:T(8,128)(2,1)S(1)}, u32[]{:S(2)}, u32[]{:S(2)}) collective-permute-start(bf16[12,2,128,128]{3,2,1,0:T(8,128)(2,1)S(1)} %broadcast_select_fusion.1), channel_id=1, source_target_pairs={{16,0},{32,16},{48,32},{64,48},{80,64},{96,80},{112,96},{128,112},... | collective-permute-start | bytes 2359304 | tf_op jit(solution)/shard_map/cond/branch_2_fun/ppermute | solution.py:27
  217.3 4.5 %copy-start.1 = (bf16[4,2,128,128]{3,2,1,0:T(8,128)(2,1)S(1)}, bf16[4,2,128,128]{3,2,1,0:T(8,128)(2,1)}, u32[]{:S(2)}) copy-start(bf16[4,2,128,128]{3,2,1,0:T(8,128)(2,1)} %get-tuple-element.56) | copy-start | bytes 786436 | tf_op jit(solution)/shard_map/cond

commit v2 on v1

--- a/solution.py
+++ b/solution.py
@@ -12,7 +12,7 @@
 START = 3
 PLAG = 3
 AHEAD = 6
-STEPS = 112
+STEPS = 110
 SIZES = (88, 104)
 
 
@@ -152,45 +152,47 @@
     return passing, jnp.minimum(first, passing[:1])
 
 
-def schedule_kernel(passing_ref, ready_ref, code_ref, sent_ref):
-    lane = lax.broadcasted_iota(jnp.int32, (1, 128), 1)
-    edge = lane % 16 == 0
-    limit = [passing_ref[i : i + 1, :] for i in range(8)]
+def schedule_kernel(passing_ref, ready_ref, code_ref, sent_ref, there_ref):
+    edge = lax.broadcasted_iota(jnp.int32, (8, 128), 1) % 16 == 0
+    limit = passing_ref[...]
     zero = jnp.zeros((1, 128), jnp.int32)
     for t in range(LAG):
         sent_ref[t] = jnp.zeros((8, 128), jnp.int32)
 
-    def slot(t, sent):
-        ready = jnp.clip((t - START + 2) // 2, 0, 24)
-        code = zero - 1
-        taken = lane < 0
-        out = []
-        for i in range(8):
-            if i == 0:
-                there = ready_ref[pl.ds(ready, 1), :]
-            else:
-                old = sent_ref[t, i - 1 : i, :]
-                there = jnp.where(edge, pltpu.roll(old, 113, 1), pltpu.roll(old, 1, 1))
-                there = jnp.minimum(there, limit[i])
-            go = (sent[i] < there) & ~taken
-            code = jnp.where(go, sent[i] + 64 * i, code)
-            taken = taken | go
-            out.append(jnp.where(go, sent[i] + 1, sent[i]))
-            sent_ref[t + LAG, i : i + 1, :] = out[i]
-        code_ref[pl.ds(t, 1), :] = code
-        return tuple(out)
-
-    lax.fori_loop(0, STEPS, slot, (zero,) * 8)
+    def group(g, sent):
+        for s in range(LAG):
+            old = sent_ref[s]
+            moved = jnp.where(edge, pltpu.roll(old, 113, 1), pltpu.roll(old, 1, 1))
+            there_ref[s] = jnp.minimum(moved, limit)
+        for s in range(LAG):
+            t = g * LAG + s
+            ready = jnp.clip((t - START + 2) // 2, 0, 24)
+            code = zero - 1
+            taken = zero
+            out = []
+            for i in range(8):
+                there = ready_ref[pl.ds(ready, 1), :] if i == 0 else there_ref[s, i - 1 : i, :]
+                go = jnp.where(sent[i] < there, 1 - taken, 0)
+                code = jnp.where(go > 0, sent[i] + 64 * i, code)
+                taken = taken + go
+                out.append(sent[i] + go)
+                sent_ref[s, i : i + 1, :] = out[i]
+            code_ref[pl.ds(t, 1), :] = code
+            sent = out
+        return tuple(sent)
+
+    lax.fori_loop(0, STEPS // LAG, group, (zero,) * 8)
 
 
 def schedule(passing, ready):
+    shifted = jnp.concatenate([passing[1:], passing[:1]], axis=0)
+    recent = jax.ShapeDtypeStruct((LAG, 8, 128), jnp.int32)
     return pl.pallas_call(
         schedule_kernel,
-        out_shape=jax.ShapeDtypeStruct((STEPS, 128), jnp.int32),
+        out_shape=(jax.ShapeDtypeStruct((STEPS, 128), jnp.int32), recent, recent),
         in_specs=[pl.BlockSpec(memory_space=pltpu.VMEM)] * 2,
-        out_specs=pl.BlockSpec(memory_space=pltpu.VMEM),
-        scratch_shapes=[pltpu.VMEM((STEPS + LAG, 8, 128), jnp.int32)],
-    )(passing, ready)
+        out_specs=(pl.BlockSpec(memory_space=pltpu.VMEM),) * 3,
+    )(shifted, ready)[0]
 
 
 def tables(owner, offsets, me):

time: 235 us -> 115 us (0.49)
  waiting for transfers between devices: 130 us -> 0 us
  Pallas kernels: 10.9 us -> 99.9 us
  starting transfers between devices: 29.9 us -> 0 us
  matrix products: 15 us -> 0 us
  loops' own time: 13.3 us -> 0.24 us
  other arithmetic: 22.5 us -> 9.88 us
  local copies, waits for them, and re-layouts: 10.1 us -> 2.48 us
    all_to_all x1 -> x0, waiting for transfers between devices: 98.6 us -> none  [general(): lax.all_to_all(outgoing, 'energy', split_axis=0, concat_axis=0, tiled=True)]
    pallas_call x1 -> x2, Pallas kernels: 10.9 us -> 99.9 us  [the longest x1 95.8 us: routed(): pl.pallas_call(functools.partial(main_kernel, size), out_shape=jax.ShapeD...]
    ppermute x4 -> x0, waiting for transfers between devices: 31.3 us -> none  [the longest x2 26.3 us: with_halo(): before = lax.ppermute(last, axis, up)]
    all_to_all x1 -> x0, starting transfers between devices: 20.3 us -> none  [general(): lax.all_to_all(outgoing, 'energy', split_axis=0, concat_axis=0, tiled=True)]
    dot_general x40 -> x0, matrix products: 15 us -> none  [the longest x4 2.8 us: batched_transposed(): jnp.einsum('jab,jcb->jac', left_block, right_block, preferred_element_typ...]
    another operation x1, loops' own time: 13.3 us -> 0.24 us  [body(): return lax.switch(choice, branches, 0)]
    ppermute x4 -> x0, starting transfers between devices: 9.56 us -> none  [the longest x2 8.1 us: with_halo(): before = lax.ppermute(last, axis, up)]
    convert_element_type x1 -> x0, other arithmetic: 4.51 us -> none  [general(): ((weight_one + 1.0) * shifted_up + weight_one * shifted_down).astype(jnp....]
  transfers between devices with their start and end apart: 5 -> 0, of which waited for: 3 -> 0; matrix products, arithmetic and copies ran while one was open for 1% -> 0% of each run, Pallas kernels for 0% -> 0%
where the time goes in v2:
time: 115 us; the launch traced here: 114 us
  Pallas kernels  99.9 us (87%)
  other arithmetic  9.88 us (9%)
  local copies, waits for them, and re-layouts  2.48 us (2%)
  between operations  1.99 us (2%)
    pallas_call x1, Pallas kernels, routed(): pl.pallas_call(functools.partial(main_kernel, size), out_shape=jax.ShapeD...  95.8 us
    pallas_call x1, Pallas kernels, schedule(): pl.pallas_call(schedule_kernel, out_shape=(jax.ShapeDtypeStruct((STEPS, 1...  4.01 us

profile of v2, /device:TPU:1, one launch (start us, length us, event | category | flops | bytes accessed | tf_op | source)
XLA Modules:
  0.0 114.5 jit_solution(3398199735620024257)
XLA Ops:
  0.0 0.7 add_select_fusion.7
  0.7 1.4 %convert_reduce_fusion.3 = (s32[384]{0:T(512)S(1)}, s32[384]{0:T(512)S(1)}, s32[384]{0:T(512)S(1)}) fusion(s32[384]{0:T(512)} %param.13, s32[384]{0:T(512)S(1)} %get-tuple-element.100, s32[384]{0:T(512)S(1)} %fusion.134), kind=kLoop, calls=%fused_computation.187 | loop fusion | flops 1915776 | bytes 9216 | tf_op jit(solution)/shard_map/reduce_sum | solution.py:138
  2.2 1.1 %select_reduce_fusion.1 = s32[32,128]{1,0:T(8,128)S(1)} fusion(s32[384]{0:T(512)S(1)} %get-tuple-element.94, pred[32,384]{1,0:T(8,128)(4,1)S(1)} %iota_compare_fusion.4, pred[128,384]{1,0:T(8,128)(4,1)S(1)} %iota_compare_fusion.3), kind=kLoop, calls=%fused_computation.182 | loop fusion | flops 4714496 | bytes 79360 | tf_op jit(solution)/shard_map/reduce_min | solution.py:151
  3.4 0.5 convert_reduce_fusion.2
  3.8 0.6 broadcast_minimum_fusion.ready_ref
  4.5 0.6 pad_add_fusion.passing_ref
  5.1 4.0 %shard_map.67 = (s32[110,128]{1,0:T(8,128)}, s32[5,8,128]{2,1,0:T(8,128)}, s32[5,8,128]{2,1,0:T(8,128)}) custom-call(s32[8,128]{1,0:T(8,128)} %pad_add_fusion.passing_ref, s32[32,128]{1,0:T(8,128)} %broadcast_minimum_fusion.ready_ref), custom_call_target="tpu_custom_call" | custom-call | tf_op jit(solution)/shard_map/pallas_call | solution.py:190
  9.1 1.2 %dynamic-slice_reduce_fusion.2 = (s32[110]{0:T(128)S(1)}, s32[110]{0:T(128)S(1)}, s32[110]{0:T(128)S(1)}) fusion(s32[110,128]{1,0:T(8,128)} %get-tuple-element.58, s32[]{:T(128)S(6)} %select_n.281, s32[]{:T(128)S(6)} %select_n.291, s32[]{:T(128)S(6)} %select_n.288), kind=kLoop, calls=%fused_computation.197 | loop fusion | bytes 2652 | tf_op jit(solution)/shard_map/dynamic_slice | solution.py:214
  10.3 0.1 select_reduce_fusion.3
  10.4 0.7 fusion.133
  11.1 0.2 select_reduce_fusion.2
  11.3 0.1 fusion.144
  11.3 0.1 pad_add_fusion.1
  11.4 0.1 dynamic_slice.45
  11.5 0.7 broadcast_compare_fusion.1
  12.2 0.1 select_reduce_fusion.5
  12.3 0.7 pad_add_fusion.2
  13.1 1.6 %select_reduce_fusion.4 = (s32[]{:T(128)}, s32[]{:T(128)}) fusion(s32[110]{0:T(128)S(1)} %iota_add_fusion.1, s32[110,128]{1,0:T(8,128)} %get-tuple-element.58), kind=kLoop, calls=%fused_computation.198 | loop fusion | flops 17598 | bytes 14528 | tf_op jit(solution)/shard_map/reduce_max | solution.py:205
  14.7 0.6 slice_reduce_fusion
  17.2 96.1 %conditional.1 = (f32[1,12,2,128,128]{4,3,2,1,0:T(8,128)S(1)}) conditional(s32[]{:T(128)} %clamp.3, (s32[174]{0:T(256)S(1)}, f32[4]{0:T(128)}, bf16[1,24,2,128,128]{4,3,2,1,0:T(8,128)(2,1)}, bf16[1,24,2,128,128]{4,3,2,1,0:T(8,128)(2,1)}, bf16[4,2,128,128]{3,2,1,0:T(8,128)(2,1)}) %tuple.14, (s32[174]{0:T(256)S(1)}, f32[4]{0:T(128)}, ...), branch_computations={%region_11.12_spmd, %region_12.13_spmd, %region_13.17_spmd} | conditional | flops 2447450624 | bytes 161513376 | solution.py:524
  17.2 95.8 %branch_0_fun.1 = f32[1,12,2,128,128]{4,3,2,1,0:T(8,128)S(1)} custom-call(s32[174]{0:T(256)S(1)} %get-tuple-element.40.table, f32[4]{0:T(128)} %get-tuple-element.42.weights, bf16[1,24,2,128,128]{4,3,2,1,0:T(8,128)(2,1)} %get-tuple-element.43.ret_hbm, bf16[1,24,2,128,128]{4,3,2,1,0:T(8,128)(2,1)} %get-tuple-element.44.sig_hbm, ...), custom_call_target="tpu_custom_call" | custom-call | tf_op jit(solution)/shard_map/cond/branch_0_fun/pallas_call | solution.py:467
  113.3 1.1 %copy.178 = f32[1,12,2,128,128]{4,3,2,1,0:T(8,128)} copy(f32[1,12,2,128,128]{4,3,2,1,0:T(8,128)S(1)} %get-tuple-element.84) | data formatting | bytes 3145728
  (12 shorter events, 0.1 us)
